TPU v7x, 128 devices: a whole 4x4x4 slice. The times are simulated.
128 devices in a mesh: req: 32 (over x, y, core), mlp: 4 (over z).
Axes of the slice: x: 4, y: 4, z: 4, core: 2. Of those that a mesh axis runs over, the one named last changes fastest.
Arguments:
- new_qkv: bfloat16 [1024, 3, 3072], P('req', None, 'mlp'), may hold values from -8 to 8
- prompt_cache: bfloat16 [32, 4096, 2, 3072], P('req', None, None, 'mlp'), may hold values from -6 to 6
- tail_cache: bfloat16 [512, 256, 2, 3072], P('req', None, None, 'mlp'), may hold values from -6 to 6
- residual: bfloat16 [1024, 3072], P('req', 'mlp'), may hold values from -6 to 6
- w_out: bfloat16 [3072, 3072], P('mlp'), may hold values from -0.109375 to 0.109375
- mlp_gain: float32 [3072], replicated, may hold values from 0.5 to 1.5
- w_gate: bfloat16 [3072, 8192], P(None, ('req', 'mlp')), may hold values from -0.109375 to 0.109375
- w_up: bfloat16 [3072, 8192], P(None, ('req', 'mlp')), may hold values from -0.109375 to 0.109375
- w_down: bfloat16 [8192, 3072], P(('req', 'mlp')), may hold values from -0.25 to 0.25
- final_gain: float32 [3072], replicated, may hold values from 0.5 to 1.5
- score_weight: float32 [3072], replicated, may hold values from -0.109375 to 0.109375
- slot_part: int32 [32], replicated, may hold values from 0 to 31, each once
- prompt_len: int32 [16], replicated, may hold values from 1 to 8192, 65536 in all
- tail_len: int32 [512], replicated, may hold values from 1 to 256, 65536 in all
Outputs:
- hidden_out: bfloat16 [1024, 3072], P('req', 'mlp')
- score: float32 [1024], P('req')
Inputs may be any that keep to these rules, and one draw needn't show every extreme that they name: Each value once; slot s holds half slot_part[s] % 2 of prompt slot_part[s] // 2. `prompt_len`: the largest is exactly 8192. `tail_len`: the largest is exactly 256.
All inputs are finite; a program needn't handle non-finite values.
Results may differ from a plain program's by a relative error of at most 0.015.
Values may be sent and summed in bfloat16 or wider, within the bound.
A program may use at most 192 MiB of HBM per device.

v0:
```python
import math
import jax
import jax.numpy as jnp
from jax import lax
from jax.sharding import PartitionSpec as P

HD = 96
norm_eps = 1e-05
masked_value = -1e30


def rotary(values, position):
    half_dim = HD // 2
    freqs = 10000.0 ** (-(jnp.arange(half_dim, dtype=jnp.float32) * 2.0) / HD)
    angles = position.astype(jnp.float32)[..., None] * freqs
    cosine = jnp.cos(angles)[..., None, :]
    sine = jnp.sin(angles)[..., None, :]
    first = values[..., :half_dim]
    second = values[..., half_dim:]
    return jnp.concatenate(
        [first * cosine - second * sine, second * cosine + first * sine], axis=-1
    )


def per_device(
    new_qkv,
    prompt_cache,
    tail_cache,
    residual,
    w_out,
    mlp_gain,
    w_gate,
    w_up,
    w_down,
    final_gain,
    score_weight,
    slot_part,
    prompt_len,
    tail_len,
):
    req_count = lax.axis_size("req")
    req_index = lax.axis_index("req")
    mlp_index = lax.axis_index("mlp")
    rows_here = new_qkv.shape[0]
    width_here = new_qkv.shape[2]
    heads_here = width_here // HD
    conts_here = rows_here // 2
    width = w_out.shape[1]
    score_scale = 1.0 / math.sqrt(HD)
    own_prompt = req_index // 2
    tail_here = lax.dynamic_slice_in_dim(tail_len, req_index * conts_here, conts_here)
    plen_here = lax.dynamic_index_in_dim(prompt_len, own_prompt, 0, keepdims=False)
    position = plen_here + tail_here[:, None] + jnp.arange(2, dtype=jnp.int32)[None, :]
    block = new_qkv.reshape(conts_here, 2, 3, heads_here, HD)
    query = rotary(block[:, :, 0].astype(jnp.float32), position).astype(jnp.bfloat16)
    key_new = rotary(block[:, :, 1].astype(jnp.float32), position).astype(jnp.bfloat16)
    value_new = block[:, :, 2]
    gathered = lax.all_gather(query.reshape(rows_here, width_here), "req", axis=0, tiled=True)
    slot_ids = jnp.arange(req_count, dtype=jnp.int32)
    slot_of = jnp.sum(
        jnp.where(slot_part[None, :] == slot_ids[:, None], slot_ids[None, :], 0), axis=1
    )
    held_part = lax.dynamic_index_in_dim(slot_part, req_index, 0, keepdims=False)
    owned_prompt = held_part // 2
    held_half = held_part % 2
    span = prompt_cache.shape[1]
    owned_rows = 2 * rows_here
    q_owned = lax.dynamic_slice_in_dim(gathered, owned_prompt * owned_rows, owned_rows, 0).reshape(
        owned_rows, heads_here, HD
    )
    owned_len = lax.dynamic_index_in_dim(prompt_len, owned_prompt, 0, keepdims=False)
    valid_count = jnp.clip(owned_len - held_half * span, 0, span)
    block_len = min(512, span)
    block_count = (valid_count + block_len - 1) // block_len
    cache_keys = prompt_cache[0, :, 0].reshape(span, heads_here, HD)
    cache_values = prompt_cache[0, :, 1].reshape(span, heads_here, HD)

    def score_block(number, buffer):
        key_block = lax.dynamic_slice_in_dim(cache_keys, number * block_len, block_len, 0)
        block_scores = (
            jnp.einsum("rhd,khd->hrk", q_owned, key_block, preferred_element_type=jnp.float32)
            * score_scale
        )
        places = number * block_len + jnp.arange(block_len, dtype=jnp.int32)
        block_scores = jnp.where(places[None, None, :] < valid_count, block_scores, masked_value)
        return lax.dynamic_update_slice_in_dim(buffer, block_scores, number * block_len, 2)

    empty_scores = jnp.full((heads_here, owned_rows, span), masked_value, jnp.float32)
    prefix_scores = lax.fori_loop(0, block_count, score_block, empty_scores)
    prefix_max = jnp.max(prefix_scores, axis=2)

    def value_block(number, carry):
        numer, totals = carry
        score_part = lax.dynamic_slice_in_dim(prefix_scores, number * block_len, block_len, 2)
        weights = jnp.exp(score_part - prefix_max[:, :, None])
        value_part = lax.dynamic_slice_in_dim(cache_values, number * block_len, block_len, 0)
        numer = numer + jnp.einsum(
            "hrk,khd->rhd",
            weights.astype(jnp.bfloat16),
            value_part,
            preferred_element_type=jnp.float32,
        )
        return (numer, totals + jnp.sum(weights, axis=2))

    start_carry = (
        jnp.zeros((owned_rows, heads_here, HD), jnp.float32),
        jnp.zeros((heads_here, owned_rows), jnp.float32),
    )
    owner_numer, owner_total = lax.fori_loop(0, block_count, value_block, start_carry)
    packed = jnp.concatenate(
        [
            owner_numer.reshape(owned_rows, width_here),
            jnp.transpose(owner_total),
            jnp.transpose(prefix_max),
        ],
        axis=1,
    )
    packed_all = lax.all_gather(packed[None], "req", axis=0, tiled=True)
    row_offset = req_index % 2 * rows_here
    slot_first = lax.dynamic_index_in_dim(slot_of, 2 * own_prompt, 0, keepdims=False)
    slot_second = lax.dynamic_index_in_dim(slot_of, 2 * own_prompt + 1, 0, keepdims=False)

    def part_of(slot):
        piece = lax.dynamic_slice_in_dim(
            lax.dynamic_index_in_dim(packed_all, slot, 0, keepdims=False), row_offset, rows_here, 0
        )
        numer = piece[:, :width_here].reshape(rows_here, heads_here, HD)
        total = piece[:, width_here : width_here + heads_here]
        top = piece[:, width_here + heads_here :]
        return (numer, total, top)

    numer_first, total_first, max_first = part_of(slot_first)
    numer_second, total_second, max_second = part_of(slot_second)
    tail_cap = tail_cache.shape[1]
    tail_keys = tail_cache[:, :, 0].reshape(conts_here, tail_cap, heads_here, HD)
    tail_values = tail_cache[:, :, 1].reshape(conts_here, tail_cap, heads_here, HD)
    s_tail = (
        jnp.einsum("cthd,cjhd->chtj", query, tail_keys, preferred_element_type=jnp.float32)
        * score_scale
    )
    s_tail = jnp.where(
        jnp.arange(tail_cap)[None, None, None, :] < tail_here[:, None, None, None],
        s_tail,
        masked_value,
    )
    s_new = (
        jnp.einsum("cthd,cuhd->chtu", query, key_new, preferred_element_type=jnp.float32)
        * score_scale
    )
    causal = jnp.arange(2)[None, :] <= jnp.arange(2)[:, None]
    s_new = jnp.where(causal[None, None, :, :], s_new, masked_value)
    tail_max = jnp.maximum(jnp.max(s_tail, -1), jnp.max(s_new, -1))
    w_tail = jnp.exp(s_tail - tail_max[..., None])
    w_new = jnp.exp(s_new - tail_max[..., None])
    numer_tail = jnp.einsum(
        "chtj,cjhd->cthd",
        w_tail.astype(jnp.bfloat16),
        tail_values,
        preferred_element_type=jnp.float32,
    )
    numer_tail = numer_tail + jnp.einsum(
        "chtu,cuhd->cthd", w_new.astype(jnp.bfloat16), value_new, preferred_element_type=jnp.float32
    )
    numer_tail = numer_tail.reshape(rows_here, heads_here, HD)
    total_tail = jnp.transpose(jnp.sum(w_tail, -1) + jnp.sum(w_new, -1), (0, 2, 1)).reshape(
        rows_here, heads_here
    )
    max_tail = jnp.transpose(tail_max, (0, 2, 1)).reshape(rows_here, heads_here)
    row_max = jnp.maximum(jnp.maximum(max_first, max_second), max_tail)
    scale_first = jnp.exp(max_first - row_max)
    scale_second = jnp.exp(max_second - row_max)
    scale_tail = jnp.exp(max_tail - row_max)
    row_total = total_first * scale_first + total_second * scale_second + total_tail * scale_tail
    row_numer = (
        numer_first * scale_first[..., None]
        + numer_second * scale_second[..., None]
        + numer_tail * scale_tail[..., None]
    )
    attn = (row_numer / row_total[:, :, None]).astype(jnp.bfloat16).reshape(rows_here, width_here)
    residual_full = lax.all_gather(residual, "mlp", axis=1, tiled=True)
    projected = lax.psum(jnp.dot(attn, w_out, preferred_element_type=jnp.float32), "mlp")
    state = residual_full.astype(jnp.float32) + projected
    mean_square = jnp.mean(state * state, axis=1, keepdims=True)
    normed = (state * lax.rsqrt(mean_square + norm_eps) * mlp_gain).astype(jnp.bfloat16)
    mlp_count = lax.axis_size("mlp")
    share = rows_here // mlp_count
    normed_share = lax.dynamic_slice_in_dim(normed, mlp_index * share, share, 0)
    piece = lax.all_gather(normed_share, "req", axis=0, tiled=True)
    gate_w = lax.all_gather(w_gate, "mlp", axis=1, tiled=True)
    up_w = lax.all_gather(w_up, "mlp", axis=1, tiled=True)
    down_w = lax.all_gather(w_down, "mlp", axis=0, tiled=True)
    gate = jnp.dot(piece, gate_w, preferred_element_type=jnp.float32)
    upper = jnp.dot(piece, up_w, preferred_element_type=jnp.float32)
    hidden_all = (jax.nn.silu(gate) * upper).astype(jnp.bfloat16)
    row_sums = lax.psum_scatter(
        jnp.dot(hidden_all, down_w, preferred_element_type=jnp.float32),
        "req",
        scatter_dimension=0,
        tiled=True,
    )
    state_share = lax.dynamic_slice_in_dim(state, mlp_index * share, share, 0)
    final_share = state_share + row_sums
    final_square = jnp.mean(final_share * final_share, axis=1)
    final_dot = jnp.sum(final_share * final_gain * score_weight, axis=1)
    score_share = final_dot * lax.rsqrt(final_square + norm_eps)
    scores = lax.all_gather(score_share, "mlp", axis=0, tiled=True)
    out_rows = lax.all_to_all(
        final_share.astype(jnp.bfloat16), "mlp", split_axis=1, concat_axis=0, tiled=True
    )
    return (out_rows, scores)


def solution(mesh):
    in_specs = (
        P("req", None, "mlp"),
        P("req", None, None, "mlp"),
        P("req", None, None, "mlp"),
        P("req", "mlp"),
        P("mlp", None),
        P(),
        P(None, ("req", "mlp")),
        P(None, ("req", "mlp")),
        P(("req", "mlp"), None),
        P(),
        P(),
        P(),
        P(),
        P(),
    )
    out_specs = (P("req", "mlp"), P("req"))
    return jax.shard_map(
        per_device, mesh=mesh, in_specs=in_specs, out_specs=out_specs, check_vma=False
    )
```

profile of v0, /device:TPU:0, one launch (start us, length us, event | category | flops | bytes accessed | tf_op | source)
XLA Modules:
  0.0 547.5 jit_solution(2006875817612300921)
XLA Ops:
  7.2 1.2 dynamic_slice.51
  11.1 1.4 fusion.47
  12.5 1.4 broadcast_add_fusion
  14.0 1.1 reshape.136
  16.0 0.7 convert_element_type.58
  17.5 24.7 %fusion.44 = (bf16[1,4096,1,768]{3,2,1,0:T(2,128)(2,1)}, bf16[1,4096,1,768]{3,2,1,0:T(2,128)(2,1)}) fusion(bf16[1,4096,2,768]{3,2,1,0:T(2,128)(2,1)} %param.19), kind=kLoop, calls=%fused_computation.90 | loop fusion | bytes 25165824 | tf_op jit(solution)/shard_map/slice | solution.py:76
  42.2 27.2 %copy.87 = bf16[1,4096,1,768]{1,3,2,0:T(8,128)(2,1)} copy(bf16[1,4096,1,768]{3,2,1,0:T(2,128)(2,1)} %get-tuple-element.154) | data formatting | bytes 12582912 | tf_op jit(solution)/shard_map/slice | solution.py:75
  69.4 27.0 %copy.86 = bf16[1,4096,1,768]{1,3,2,0:T(8,128)(2,1)} copy(bf16[1,4096,1,768]{3,2,1,0:T(2,128)(2,1)} %get-tuple-element.153) | data formatting | bytes 12582912 | tf_op jit(solution)/shard_map/slice | solution.py:76
  96.4 0.9 constant_dynamic-slice_fusion
  97.5 4.2 broadcast_in_dim.60
  101.8 9.7 %while.22 = (s32[]{:T(128)}, f32[8,64,4096]{2,1,0:T(8,128)}, s32[]{:T(128)}, s32[]{:T(128)}, bf16[4096,8,96]{0,2,1:T(8,128)(2,1)}, /*index=5*/bf16[64,8,96]{2,0,...) while((s32[]{:T(128)}, f32[8,64,4096]{2,1,0:T(8,128)}, s32[]{:T(128)}, s32[]{:T(128)}, ...), condition=%wide.region_1.2_spmd, body=%wide.region_0.1_spmd.sunk | while | flops 50856964 | bytes 1935515 | solution.py:89
  101.8 2.4 fusion.71
  104.2 2.4 fusion.71
  106.6 2.4 fusion.71
  109.0 2.4 fusion.71
  111.4 3.8 reduce_max.27
  115.3 14.2 %while.23 = (s32[]{:T(128)}, f32[64,8,96]{2,0,1:T(8,128)S(1)}, f32[8,64]{1,0:T(8,128)S(1)}, s32[]{:T(128)}, bf16[4096,8,96]{0,2,1:T(8,128)(2,1)}, /*index=5*/f32...) while((s32[]{:T(128)}, f32[64,8,96]{2,0,1:T(8,128)S(1)}, ...), condition=%wide.region_5.6_spmd, body=%wide.region_3.5_spmd.sunk | while | flops 51429380 | bytes 3290271 | solution.py:109
  115.4 1.9 fusion.74
  117.3 1.6 fusion.75
  118.9 1.9 fusion.74
  120.8 1.6 fusion.75
  122.4 1.9 fusion.74
  124.4 1.6 fusion.75
  126.0 1.9 fusion.74
  127.9 1.6 fusion.75
  130.0 0.8 pad_maximum_fusion
  134.1 25.7 %fusion.43 = (bf16[16,256,1,768]{3,2,1,0:T(2,128)(2,1)}, bf16[16,256,1,768]{3,2,1,0:T(2,128)(2,1)}) fusion(bf16[16,256,2,768]{3,2,1,0:T(2,128)(2,1)} %param.20), kind=kLoop, calls=%fused_computation.89 | loop fusion | bytes 25165824 | tf_op jit(solution)/shard_map/slice | solution.py:136
  159.9 29.2 %copy.94 = bf16[16,256,1,768]{1,3,0,2:T(8,128)(2,1)} copy(bf16[16,256,1,768]{3,2,1,0:T(2,128)(2,1)} %get-tuple-element.152) | data formatting | bytes 12582912 | tf_op jit(solution)/shard_map/slice | solution.py:135
  190.1 3.8 fusion.48
  194.3 29.2 %copy.99 = bf16[16,256,1,768]{1,3,0,2:T(8,128)(2,1)} copy(bf16[16,256,1,768]{3,2,1,0:T(2,128)(2,1)} %get-tuple-element.151) | data formatting | bytes 12582912 | tf_op jit(solution)/shard_map/slice | solution.py:136
  223.8 4.6 fusion.15
  230.7 1.0 dynamic-slice_bitcast_fusion.1
  232.6 4.0 fusion.34
  237.3 13.5 %all_gather.24 = bf16[32,3072]{1,0:T(8,128)(2,1)S(1)} all-gather(bf16[32,768]{1,0:T(8,128)(2,1)S(1)} %copy-done), channel_id=1, replica_groups=mesh['req'=32,'mlp'=4] {'mlp'}, dimensions={1}, use_global_device_ids=true | all-gather | bytes 245760 | tf_op jit(solution)/shard_map/all_gather | solution.py:180
  250.7 54.6 %all-reduce.3.cloned.1.call-done = f32[32,3072]{1,0:T(8,128)} async-done(((f32[32,3072]{1,0:T(8,128)}), f32[32,3072]{1,0:T(8,128)}) %all-reduce.3.cloned.1.call-update) | async-done | bytes 393232 | tf_op jit(solution)/shard_map/psum | solution.py:181
  305.3 1.2 multiply_reduce_fusion
  306.5 0.7 multiply_convert_fusion
  307.9 0.7 all-gather.16.cloned.1.call-update
  308.7 25.4 %all-gather.12.cloned.1.call-done = bf16[3072,256]{0,1:T(8,128)(2,1)} async-done(((bf16[3072,64]{0,1:T(8,128)(2,1)}), bf16[3072,256]{0,1:T(8,128)(2,1)}) %all-gather.12.cloned.1.call-update) | async-done | bytes 1572880 | tf_op jit(solution)/shard_map/all_gather | solution.py:189
  334.0 46.0 %all-gather.10.cloned.1.call-done = bf16[256,3072]{1,0:T(8,128)(2,1)} async-done(((bf16[8,3072]{1,0:T(8,128)(2,1)}), bf16[256,3072]{1,0:T(8,128)(2,1)}) %all-gather.10.cloned.1.call-update) | async-done | bytes 1572880 | tf_op jit(solution)/shard_map/all_gather | solution.py:188
  380.0 2.5 fusion.49
  382.5 25.2 %all-gather.14.cloned.1.call-done = bf16[3072,256]{0,1:T(8,128)(2,1)} async-done(((bf16[3072,64]{0,1:T(8,128)(2,1)}), bf16[3072,256]{0,1:T(8,128)(2,1)}) %all-gather.14.cloned.1.call-update) | async-done | bytes 1572880 | tf_op jit(solution)/shard_map/all_gather | solution.py:190
  407.8 28.5 %all-gather.16.cloned.1.call-done = bf16[256,3072]{1,0:T(8,128)(2,1)} async-done(((bf16[64,3072]{1,0:T(8,128)(2,1)}), bf16[256,3072]{1,0:T(8,128)(2,1)}) %all-gather.16.cloned.1.call-update) | async-done | bytes 1572880 | tf_op jit(solution)/shard_map/all_gather | solution.py:191
  436.2 5.8 %fusion.14 = f32[256,3072]{1,0:T(8,128)} fusion(bf16[256,3072]{1,0:T(8,128)(2,1)} %all-gather.16.cloned.1.call-done, bf16[256,3072]{1,0:T(8,128)(2,1)} %all-gather.10.cloned.1.call-done, bf16[3072,256]{0,1:T(8,128)(2,1)} %all-gather.14.cloned.1.call-done, f32[256,256]{1,0:T(8,128)S(1)} %fusion.49), kind=kOutput, calls=%fused_computation.19 | convolution fusion | flops 805699584 | bytes 8126464 | tf_op jit(solution)/shard_map/dot_general | solution.py:196
  443.4 79.1 %reduce-scatter.2.cloned.1.call-done = f32[8,3072]{1,0:T(8,128)} async-done(((f32[256,3072]{1,0:T(8,128)}), f32[8,3072]{1,0:T(8,128)}) %reduce-scatter.2.cloned.1.call-update) | async-done | bytes 98320 | tf_op jit(solution)/shard_map/reduce_scatter | solution.py:195
  522.4 1.7 multiply_reduce_fusion.1
  524.1 4.4 all-to-all-start
  528.6 11.4 %all-reduce = f32[32]{0:T(128)} all-reduce(f32[32]{0:T(128)S(1)} %multiply_dynamic-update-slice_fusion), channel_id=1, replica_groups=mesh['req'=32,'mlp'=4] {'mlp'}, use_global_device_ids=true, to_apply=%add | all-reduce | flops 32 | bytes 256
  (90 shorter events, 8.7 us)
Async XLA Ops:
  7.2 89.3 %all-gather.8.cloned.1.call-start = ((), (), s32[]{:S(2)}) async-start(), calls=%async_computation.2 | async-start | bytes 1622016 | tf_op jit(solution)/shard_map/all_gather | solution.py:58
  16.8 213.9 %all-gather.18.cloned.1.call-start = ((), (), s32[]{:S(2)}) async-start(), calls=%async_computation.9 | async-start | bytes 7569408 | tf_op jit(solution)/shard_map/all_gather | solution.py:118
  115.3 15.5 %copy-start.4 = (s32[32]{0:T(128)S(1)}, s32[32]{0:T(128)}, u32[]{:S(2)}) copy-start(s32[32]{0:T(128)} %param.29) | copy-start | bytes 388
  130.8 174.5 %all-reduce.3.cloned.1.call-start = ((), (), s32[]{:S(2)}) async-start(), calls=%async_computation.3 | async-start | bytes 786432 | tf_op jit(solution)/shard_map/psum | solution.py:181
  228.4 8.9 %copy-start = (bf16[32,768]{1,0:T(8,128)(2,1)S(1)}, bf16[32,768]{1,0:T(8,128)(2,1)}, u32[]{:S(2)}) copy-start(bf16[32,768]{1,0:T(8,128)(2,1)} %param.21) | copy-start | bytes 147460
  228.4 78.2 %copy-start.3 = (f32[3072]{0:T(1024)S(1)}, f32[3072]{0:T(1024)}, u32[]{:S(2)}) copy-start(f32[3072]{0:T(1024)} %param.23) | copy-start | bytes 36868
  236.6 97.4 %all-gather.12.cloned.1.call-start = ((), (), s32[]{:S(2)}) async-start(), calls=%async_computation.5 | async-start | bytes 1966080 | tf_op jit(solution)/shard_map/all_gather | solution.py:189
  237.2 142.8 %all-gather.10.cloned.1.call-start = ((), (), s32[]{:S(2)}) async-start(), calls=%async_computation.4 | async-start | bytes 1622016 | tf_op jit(solution)/shard_map/all_gather | solution.py:188
  307.3 100.5 %all-gather.14.cloned.1.call-start = ((), (), s32[]{:S(2)}) async-start(), calls=%async_computation.6 | async-start | bytes 1966080 | tf_op jit(solution)/shard_map/all_gather | solution.py:190
  307.9 128.4 %all-gather.16.cloned.1.call-start = ((), (), s32[]{:S(2)}) async-start(), calls=%async_computation.7 | async-start | bytes 1966080 | tf_op jit(solution)/shard_map/all_gather | solution.py:191
  308.6 213.8 %reduce-scatter.2.cloned.1.call-start = ((), (), s32[]{:S(2)}) async-start(), calls=%async_computation.8 | async-start | bytes 3244032 | tf_op jit(solution)/shard_map/reduce_scatter | solution.py:195
  382.5 59.6 %copy-start.5 = (u32[128]{0:T(128)S(1)}, u32[128]{0:T(128)}, u32[]{:S(2)}) copy-start(u32[128]{0:T(128)} %constant.186) | copy-start | bytes 1540
  382.5 139.9 %copy-start.1 = (f32[3072]{0:T(1024)S(1)}, f32[3072]{0:T(1024)}, u32[]{:S(2)}) copy-start(f32[3072]{0:T(1024)} %param.28) | copy-start | bytes 36868
  382.5 139.9 %copy-start.2 = (f32[3072]{0:T(1024)S(1)}, f32[3072]{0:T(1024)}, u32[]{:S(2)}) copy-start(f32[3072]{0:T(1024)} %param.27) | copy-start | bytes 36868
  524.1 16.0 %all-to-all-start = ((bf16[8,4,768]{2,0,1:T(8,128)(2,1)}), bf16[8,4,768]{2,0,1:T(8,128)(2,1)S(1)}, u32[]{:S(2)}, u32[]{:S(2)}) async-start(bf16[8,4,768]{2,0,1:T(8,128)(2,1)} %bitcast.26), calls=%async_computation.1 | async-start | bytes 98304 | tf_op jit(solution)/shard_map/all_to_all | solution.py:207
Sparse Core Ops, SparseCore 0:
  16.9 45.5 all-gather.7
  130.9 76.9 all-gather.17
  236.7 68.5 all-reduce.2
  306.9 27.0 all-gather.11
  337.0 43.0 all-gather.9
  381.6 26.1 all-gather.13
  409.5 26.6 all-gather.15
  442.2 80.1 reduce-scatter.1
where the time goes:
time: 552 us; the launch traced here: 548 us
  waiting for transfers between devices  261 us (47%)
  local copies, waits for them, and re-layouts  178 us (32%)
  matrix products  38.7 us (7%)
  blocking collectives  24.9 us (5%)
  between operations  22.4 us (4%)
  other arithmetic  17.9 us (3%)
    reduce_scatter x1, waiting for transfers between devices, per_device(): lax.psum_scatter(jnp.dot(hidden_all, down_w, preferred_element_type=jnp.f...  79.1 us
    slice x2, local copies, waits for them, and re-layouts, per_device(): tail_cache[:, :, 1].reshape(conts_here, tail_cap, heads_here, HD)  54.9 us
    psum x1, waiting for transfers between devices, per_device(): lax.psum(jnp.dot(attn, w_out, preferred_element_type=jnp.float32), 'mlp')  54.6 us
    slice x2, local copies, waits for them, and re-layouts, per_device(): cache_values = prompt_cache[0, :, 1].reshape(span, heads_here, HD)  51.7 us
    all_gather x1, waiting for transfers between devices, per_device(): piece = lax.all_gather(normed_share, 'req', axis=0, tiled=True)  46 us
    slice x1, local copies, waits for them, and re-layouts, per_device(): tail_cache[:, :, 0].reshape(conts_here, tail_cap, heads_here, HD)  29.2 us
    all_gather x1, waiting for transfers between devices, per_device(): down_w = lax.all_gather(w_down, 'mlp', axis=0, tiled=True)  28.5 us
    slice x1, local copies, waits for them, and re-layouts, per_device(): cache_keys = prompt_cache[0, :, 0].reshape(span, heads_here, HD)  27.2 us
  transfers between devices with their start and end apart: 9, of which 6 were waited for; matrix products, arithmetic and copies ran while one was open for 33% of the time, Pallas kernels for 0%

commit v1 on v0

--- a/solution.py
+++ b/solution.py
@@ -178,7 +178,9 @@
     )
     attn = (row_numer / row_total[:, :, None]).astype(jnp.bfloat16).reshape(rows_here, width_here)
     residual_full = lax.all_gather(residual, "mlp", axis=1, tiled=True)
-    projected = lax.psum(jnp.dot(attn, w_out, preferred_element_type=jnp.float32), "mlp")
+    projected = jnp.sum(
+        lax.all_gather(jnp.dot(attn, w_out, preferred_element_type=jnp.float32), "mlp"), axis=0
+    )
     state = residual_full.astype(jnp.float32) + projected
     mean_square = jnp.mean(state * state, axis=1, keepdims=True)
     normed = (state * lax.rsqrt(mean_square + norm_eps) * mlp_gain).astype(jnp.bfloat16)

time: 552 us -> 535 us (0.969)
  waiting for transfers between devices: 261 us -> 243 us
    psum x1 -> x0, waiting for transfers between devices: 54.6 us -> none  [per_device(): lax.psum(jnp.dot(attn, w_out, preferred_element_type=jnp.float32), 'mlp')]
    all_gather x0 -> x1, waiting for transfers between devices: none -> 38.9 us  [per_device(): lax.all_gather(jnp.dot(attn, w_out, preferred_element_type=jnp.float32),...]
  transfers between devices with their start and end apart: 9 -> 9, of which waited for: 6 -> 6; matrix products, arithmetic and copies ran while one was open for 33% -> 34% of each run, Pallas kernels for 0% -> 0%
where the time goes in v1:
time: 535 us; the launch traced here: 531 us
  waiting for transfers between devices  243 us (45%)
  local copies, waits for them, and re-layouts  178 us (33%)
  matrix products  38.7 us (7%)
  blocking collectives  24.9 us (5%)
  between operations  22.4 us (4%)
  other arithmetic  18.5 us (3%)
    reduce_scatter x1, waiting for transfers between devices, per_device(): lax.psum_scatter(jnp.dot(hidden_all, down_w, preferred_element_type=jnp.f...  79.1 us
    slice x2, local copies, waits for them, and re-layouts, per_device(): tail_cache[:, :, 1].reshape(conts_here, tail_cap, heads_here, HD)  54.9 us
    slice x2, local copies, waits for them, and re-layouts, per_device(): cache_values = prompt_cache[0, :, 1].reshape(span, heads_here, HD)  51.7 us
    all_gather x1, waiting for transfers between devices, per_device(): piece = lax.all_gather(normed_share, 'req', axis=0, tiled=True)  45.7 us
    all_gather x1, waiting for transfers between devices, per_device(): lax.all_gather(jnp.dot(attn, w_out, preferred_element_type=jnp.float32),...  38.9 us
    slice x1, local copies, waits for them, and re-layouts, per_device(): tail_cache[:, :, 0].reshape(conts_here, tail_cap, heads_here, HD)  29.2 us
    all_gather x1, waiting for transfers between devices, per_device(): down_w = lax.all_gather(w_down, 'mlp', axis=0, tiled=True)  28.4 us
    slice x1, local copies, waits for them, and re-layouts, per_device(): cache_keys = prompt_cache[0, :, 0].reshape(span, heads_here, HD)  27.2 us
  transfers between devices with their start and end apart: 9, of which 6 were waited for; matrix products, arithmetic and copies ran while one was open for 34% of the time, Pallas kernels for 0%

profile of v1, /device:TPU:0, one launch (start us, length us, event | category | flops | bytes accessed | tf_op | source)
XLA Modules:
  0.0 530.9 jit_solution(18153645477585577493)
XLA Ops:
  7.2 1.2 dynamic_slice.51
  11.1 1.4 fusion.47
  12.5 1.4 broadcast_add_fusion
  14.0 1.1 reshape.136
  16.0 0.7 convert_element_type.58
  17.5 24.7 %fusion.44 = (bf16[1,4096,1,768]{3,2,1,0:T(2,128)(2,1)}, bf16[1,4096,1,768]{3,2,1,0:T(2,128)(2,1)}) fusion(bf16[1,4096,2,768]{3,2,1,0:T(2,128)(2,1)} %param.19), kind=kLoop, calls=%fused_computation.90 | loop fusion | bytes 25165824 | tf_op jit(solution)/shard_map/slice | solution.py:76
  42.2 27.2 %copy.87 = bf16[1,4096,1,768]{1,3,2,0:T(8,128)(2,1)} copy(bf16[1,4096,1,768]{3,2,1,0:T(2,128)(2,1)} %get-tuple-element.154) | data formatting | bytes 12582912 | tf_op jit(solution)/shard_map/slice | solution.py:75
  69.4 27.0 %copy.86 = bf16[1,4096,1,768]{1,3,2,0:T(8,128)(2,1)} copy(bf16[1,4096,1,768]{3,2,1,0:T(2,128)(2,1)} %get-tuple-element.153) | data formatting | bytes 12582912 | tf_op jit(solution)/shard_map/slice | solution.py:76
  96.4 0.9 constant_dynamic-slice_fusion
  97.5 4.2 broadcast_in_dim.60
  101.8 9.7 %while.22 = (s32[]{:T(128)}, f32[8,64,4096]{2,1,0:T(8,128)}, s32[]{:T(128)}, s32[]{:T(128)}, bf16[4096,8,96]{0,2,1:T(8,128)(2,1)}, /*index=5*/bf16[64,8,96]{2,0,...) while((s32[]{:T(128)}, f32[8,64,4096]{2,1,0:T(8,128)}, s32[]{:T(128)}, s32[]{:T(128)}, ...), condition=%wide.region_1.2_spmd, body=%wide.region_0.1_spmd.sunk | while | flops 50856964 | bytes 1935515 | solution.py:89
  101.8 2.4 fusion.71
  104.2 2.4 fusion.71
  106.6 2.4 fusion.71
  109.0 2.4 fusion.71
  111.4 3.8 reduce_max.27
  115.3 14.2 %while.23 = (s32[]{:T(128)}, f32[64,8,96]{2,0,1:T(8,128)S(1)}, f32[8,64]{1,0:T(8,128)S(1)}, s32[]{:T(128)}, bf16[4096,8,96]{0,2,1:T(8,128)(2,1)}, /*index=5*/f32...) while((s32[]{:T(128)}, f32[64,8,96]{2,0,1:T(8,128)S(1)}, ...), condition=%wide.region_5.6_spmd, body=%wide.region_3.5_spmd.sunk | while | flops 51429380 | bytes 3290271 | solution.py:109
  115.4 1.9 fusion.74
  117.3 1.6 fusion.75
  118.9 1.9 fusion.74
  120.8 1.6 fusion.75
  122.4 1.9 fusion.74
  124.4 1.6 fusion.75
  126.0 1.9 fusion.74
  127.9 1.6 fusion.75
  130.0 0.8 pad_maximum_fusion
  134.1 25.7 %fusion.43 = (bf16[16,256,1,768]{3,2,1,0:T(2,128)(2,1)}, bf16[16,256,1,768]{3,2,1,0:T(2,128)(2,1)}) fusion(bf16[16,256,2,768]{3,2,1,0:T(2,128)(2,1)} %param.20), kind=kLoop, calls=%fused_computation.89 | loop fusion | bytes 25165824 | tf_op jit(solution)/shard_map/slice | solution.py:136
  159.9 29.2 %copy.94 = bf16[16,256,1,768]{1,3,0,2:T(8,128)(2,1)} copy(bf16[16,256,1,768]{3,2,1,0:T(2,128)(2,1)} %get-tuple-element.152) | data formatting | bytes 12582912 | tf_op jit(solution)/shard_map/slice | solution.py:135
  190.1 3.8 fusion.48
  194.3 29.2 %copy.99 = bf16[16,256,1,768]{1,3,0,2:T(8,128)(2,1)} copy(bf16[16,256,1,768]{3,2,1,0:T(2,128)(2,1)} %get-tuple-element.151) | data formatting | bytes 12582912 | tf_op jit(solution)/shard_map/slice | solution.py:136
  223.8 4.6 fusion.15
  230.7 1.0 dynamic-slice_bitcast_fusion.1
  232.6 4.0 fusion.34
  237.3 13.5 %all_gather.30 = bf16[32,3072]{1,0:T(8,128)(2,1)S(1)} all-gather(bf16[32,768]{1,0:T(8,128)(2,1)S(1)} %copy-done), channel_id=1, replica_groups=mesh['req'=32,'mlp'=4] {'mlp'}, dimensions={1}, use_global_device_ids=true | all-gather | bytes 245760 | tf_op jit(solution)/shard_map/all_gather | solution.py:180
  250.7 38.9 %all-gather.22.cloned.1.call-done = f32[128,3072]{1,0:T(8,128)} async-done(((f32[32,3072]{1,0:T(8,128)}), f32[128,3072]{1,0:T(8,128)}) %all-gather.22.cloned.1.call-update) | async-done | bytes 1572880 | tf_op jit(solution)/shard_map/all_gather | solution.py:182
  289.6 1.5 reduce_sum.75
  291.4 0.7 multiply_convert_fusion
  292.8 0.7 all-gather.18.cloned.1.call-update
  293.5 24.3 %all-gather.14.cloned.1.call-done = bf16[3072,256]{0,1:T(8,128)(2,1)} async-done(((bf16[3072,64]{0,1:T(8,128)(2,1)}), bf16[3072,256]{0,1:T(8,128)(2,1)}) %all-gather.14.cloned.1.call-update) | async-done | bytes 1572880 | tf_op jit(solution)/shard_map/all_gather | solution.py:191
  317.8 45.7 %all-gather.12.cloned.1.call-done = bf16[256,3072]{1,0:T(8,128)(2,1)} async-done(((bf16[8,3072]{1,0:T(8,128)(2,1)}), bf16[256,3072]{1,0:T(8,128)(2,1)}) %all-gather.12.cloned.1.call-update) | async-done | bytes 1572880 | tf_op jit(solution)/shard_map/all_gather | solution.py:190
  363.5 2.5 fusion.49
  366.1 25.1 %all-gather.16.cloned.1.call-done = bf16[3072,256]{0,1:T(8,128)(2,1)} async-done(((bf16[3072,64]{0,1:T(8,128)(2,1)}), bf16[3072,256]{0,1:T(8,128)(2,1)}) %all-gather.16.cloned.1.call-update) | async-done | bytes 1572880 | tf_op jit(solution)/shard_map/all_gather | solution.py:192
  391.2 28.4 %all-gather.18.cloned.1.call-done = bf16[256,3072]{1,0:T(8,128)(2,1)} async-done(((bf16[64,3072]{1,0:T(8,128)(2,1)}), bf16[256,3072]{1,0:T(8,128)(2,1)}) %all-gather.18.cloned.1.call-update) | async-done | bytes 1572880 | tf_op jit(solution)/shard_map/all_gather | solution.py:193
  419.6 5.8 %fusion.14 = f32[256,3072]{1,0:T(8,128)} fusion(bf16[256,3072]{1,0:T(8,128)(2,1)} %all-gather.18.cloned.1.call-done, bf16[256,3072]{1,0:T(8,128)(2,1)} %all-gather.12.cloned.1.call-done, bf16[3072,256]{0,1:T(8,128)(2,1)} %all-gather.16.cloned.1.call-done, f32[256,256]{1,0:T(8,128)S(1)} %fusion.49), kind=kOutput, calls=%fused_computation.19 | convolution fusion | flops 805699584 | bytes 8126464 | tf_op jit(solution)/shard_map/dot_general | solution.py:198
  426.7 79.1 %reduce-scatter.2.cloned.1.call-done = f32[8,3072]{1,0:T(8,128)} async-done(((f32[256,3072]{1,0:T(8,128)}), f32[8,3072]{1,0:T(8,128)}) %reduce-scatter.2.cloned.1.call-update) | async-done | bytes 98320 | tf_op jit(solution)/shard_map/reduce_scatter | solution.py:197
  505.8 1.7 multiply_reduce_fusion.1
  507.4 4.4 all-to-all-start
  512.0 11.4 %all-reduce = f32[32]{0:T(128)} all-reduce(f32[32]{0:T(128)S(1)} %multiply_dynamic-update-slice_fusion), channel_id=1, replica_groups=mesh['req'=32,'mlp'=4] {'mlp'}, use_global_device_ids=true, to_apply=%add | all-reduce | flops 32 | bytes 256
  (91 shorter events, 8.9 us)
Async XLA Ops:
  7.2 89.3 %all-gather.10.cloned.1.call-start = ((), (), s32[]{:S(2)}) async-start(), calls=%async_computation.2 | async-start | bytes 1622016 | tf_op jit(solution)/shard_map/all_gather | solution.py:58
  16.8 213.9 %all-gather.20.cloned.1.call-start = ((), (), s32[]{:S(2)}) async-start(), calls=%async_computation.8 | async-start | bytes 7569408 | tf_op jit(solution)/shard_map/all_gather | solution.py:118
  115.3 15.5 %copy-start.4 = (s32[32]{0:T(128)S(1)}, s32[32]{0:T(128)}, u32[]{:S(2)}) copy-start(s32[32]{0:T(128)} %param.29) | copy-start | bytes 388
  130.8 158.9 %all-gather.22.cloned.1.call-start = ((), (), s32[]{:S(2)}) async-start(), calls=%async_computation.9 | async-start | bytes 1966080 | tf_op jit(solution)/shard_map/all_gather | solution.py:182
  228.4 8.9 %copy-start = (bf16[32,768]{1,0:T(8,128)(2,1)S(1)}, bf16[32,768]{1,0:T(8,128)(2,1)}, u32[]{:S(2)}) copy-start(bf16[32,768]{1,0:T(8,128)(2,1)} %param.21) | copy-start | bytes 147460
  228.6 62.8 %copy-start.3 = (f32[3072]{0:T(1024)S(1)}, f32[3072]{0:T(1024)}, u32[]{:S(2)}) copy-start(f32[3072]{0:T(1024)} %param.23) | copy-start | bytes 36868
  236.6 81.2 %all-gather.14.cloned.1.call-start = ((), (), s32[]{:S(2)}) async-start(), calls=%async_computation.4 | async-start | bytes 1966080 | tf_op jit(solution)/shard_map/all_gather | solution.py:191
  237.2 126.3 %all-gather.12.cloned.1.call-start = ((), (), s32[]{:S(2)}) async-start(), calls=%async_computation.3 | async-start | bytes 1622016 | tf_op jit(solution)/shard_map/all_gather | solution.py:190
  292.1 99.1 %all-gather.16.cloned.1.call-start = ((), (), s32[]{:S(2)}) async-start(), calls=%async_computation.5 | async-start | bytes 1966080 | tf_op jit(solution)/shard_map/all_gather | solution.py:192
  292.7 126.9 %all-gather.18.cloned.1.call-start = ((), (), s32[]{:S(2)}) async-start(), calls=%async_computation.6 | async-start | bytes 1966080 | tf_op jit(solution)/shard_map/all_gather | solution.py:193
  293.5 212.3 %reduce-scatter.2.cloned.1.call-start = ((), (), s32[]{:S(2)}) async-start(), calls=%async_computation.7 | async-start | bytes 3244032 | tf_op jit(solution)/shard_map/reduce_scatter | solution.py:197
  366.0 59.4 %copy-start.5 = (u32[128]{0:T(128)S(1)}, u32[128]{0:T(128)}, u32[]{:S(2)}) copy-start(u32[128]{0:T(128)} %constant.186) | copy-start | bytes 1540
  366.1 139.7 %copy-start.1 = (f32[3072]{0:T(1024)S(1)}, f32[3072]{0:T(1024)}, u32[]{:S(2)}) copy-start(f32[3072]{0:T(1024)} %param.28) | copy-start | bytes 36868
  366.1 139.7 %copy-start.2 = (f32[3072]{0:T(1024)S(1)}, f32[3072]{0:T(1024)}, u32[]{:S(2)}) copy-start(f32[3072]{0:T(1024)} %param.27) | copy-start | bytes 36868
  507.4 16.0 %all-to-all-start = ((bf16[8,4,768]{2,0,1:T(8,128)(2,1)}), bf16[8,4,768]{2,0,1:T(8,128)(2,1)S(1)}, u32[]{:S(2)}, u32[]{:S(2)}) async-start(bf16[8,4,768]{2,0,1:T(8,128)(2,1)} %bitcast.27), calls=%async_computation.1 | async-start | bytes 98304 | tf_op jit(solution)/shard_map/all_to_all | solution.py:209
Sparse Core Ops, SparseCore 0:
  16.9 45.5 all-gather.9
  130.9 76.9 all-gather.19
  236.8 52.8 all-gather.21
  291.1 26.6 all-gather.13
  320.5 43.0 all-gather.11
  365.1 26.1 all-gather.15
  392.9 26.6 all-gather.17
  425.6 80.1 reduce-scatter.1
